TPU v7x, 32 devices: a whole 2x2x4 slice. The times are simulated.
32 devices in a mesh: parts: 2 (over y), space: 16 (over z, x, core).
Axes of the slice: x: 2, y: 2, z: 4, core: 2. Of those that a mesh axis runs over, the one named last changes fastest.
Arguments:
- snapshots: bfloat16 [2176, 8192], P('space', 'parts'), parts along dimension 1
- starts: int32 [16], replicated, may hold values from 0 to 1920, as said below
- bins: int32 [32], replicated, may hold values from 0 to 128
- mode_count: int32 [32], replicated, may hold values from 4 to 16
Outputs:
- modes: bfloat16 [32, 32, 8192], P(None, None, ('parts', 'space')), parts along dimension 2
- factor: float32 [64, 32, 32], P('parts'), parts along dimension 0
There are 2 independent parts, one for each index of `parts`. A program takes and returns all parts, laid end to end along the dimension named above; an argument that names none is the same for every part. Nothing has to cross between parts.
Inputs may be any that keep to these rules, and one draw needn't show every extreme that they name: Block starts rise; the first block starts at 0, the last at 1920, and successive starts differ by 64 to 192 snapshots.
All inputs are finite; a program needn't handle non-finite values.
Results may differ from a plain program's by a relative error of at most 0.008.
Values may be sent and summed in bfloat16 or wider, within the bound.
No kernel may reach another device: no remote copies, remote signals or barrier semaphores. Data moves between devices by JAX's collectives and lax.ppermute only.
A program may use at most 64 MiB of HBM per device.

v0:
```python
import math

import jax
import jax.numpy as jnp
from jax import lax
from jax.sharding import PartitionSpec as P

NB = 16
NWIN = 256
NFREQ = 32


def make_table(bins):
    offsets = jnp.arange(NWIN, dtype=jnp.int32)
    window = 0.5 - 0.5 * jnp.cos(2.0 * math.pi * offsets.astype(jnp.float32) / NWIN)
    scaling = 1.0 / jnp.sqrt(jnp.sum(window * window))
    turns = bins[:, None] * offsets[None, :] % NWIN
    phases = 2.0 * math.pi * turns.astype(jnp.float32) / NWIN
    cos_rows = scaling * window[None, :] * jnp.cos(phases)
    sin_rows = -scaling * window[None, :] * jnp.sin(phases)
    return jnp.concatenate([cos_rows, sin_rows], axis=0).astype(jnp.bfloat16)


def on_device(snapshots, starts, bins, mode_count):
    time_dev, all_points = snapshots.shape
    groups = lax.axis_size("space")
    points_dev = all_points // groups
    fourier_table = make_table(bins)
    arranged = snapshots.reshape(time_dev, groups, points_dev)
    series = lax.all_to_all(arranged, "space", split_axis=1, concat_axis=0, tiled=True)[:, 0, :]
    time_mean = jnp.mean(series.astype(jnp.float32), axis=0)
    centered = (series.astype(jnp.float32) - time_mean[None, :]).astype(jnp.bfloat16)

    def take_block(first):
        return lax.dynamic_slice_in_dim(centered, first, NWIN, 0)

    welch_windows = jax.vmap(take_block)(starts)
    matrix_product = jnp.einsum(
        "vx,oxy->voy", fourier_table, welch_windows, preferred_element_type=jnp.float32
    )
    spectra = matrix_product.astype(jnp.bfloat16)
    real_component = spectra[:NFREQ]
    imag_part = spectra[NFREQ:]
    stacked = jnp.concatenate([real_component, imag_part], axis=1)
    local_gram = jnp.einsum("fip,fjp->fij", stacked, stacked, preferred_element_type=jnp.float32)
    gram = lax.psum(local_gram, "space")
    real_real = gram[:, :NB, :NB]
    real_imag = gram[:, :NB, NB:]
    imag_real = gram[:, NB:, :NB]
    imag_imag = gram[:, NB:, NB:]
    summed = real_real + imag_imag
    skew_part = real_imag - imag_real
    upper_rows = jnp.concatenate([summed, -skew_part], axis=2)
    lower_rows = jnp.concatenate([skew_part, summed], axis=2)
    cross = jnp.concatenate([upper_rows, lower_rows], axis=1) / jnp.float32(all_points)
    lower_cholesky_matrix = jnp.linalg.cholesky(cross)
    signed = jnp.concatenate([real_component, -imag_part], axis=1).astype(jnp.float32)

    def solve_one(matrix, values):
        return jax.scipy.linalg.solve_triangular(matrix, values, lower=True)

    basis = jax.vmap(solve_one)(lower_cholesky_matrix, signed)
    row_index = jnp.arange(2 * NB, dtype=jnp.int32) % NB
    keep = row_index[None, :, None] < mode_count[:, None, None]
    modes = jnp.where(keep, basis, jnp.zeros_like(basis)).astype(jnp.bfloat16)
    factor = jnp.swapaxes(lower_cholesky_matrix, 1, 2)
    return (modes, factor)


def solution(mesh):
    in_specs = (P("space", "parts"), P(), P(), P())
    out_specs = (P(None, None, ("parts", "space")), P("parts", None, None))
    return jax.shard_map(
        on_device, mesh=mesh, in_specs=in_specs, out_specs=out_specs, check_vma=False
    )
```

profile of v0, /device:TPU:0, one launch (start us, length us, event | category | flops | bytes accessed | tf_op | source)
XLA Modules:
  0.0 287.9 jit_solution(15959052177133936224)
XLA Ops:
  7.2 2.4 copy.33
  9.5 7.4 %all-to-all-start = ((bf16[136,16,256]{2,0,1:T(8,128)(2,1)}), bf16[136,16,256]{2,0,1:T(8,128)(2,1)S(1)}, u32[]{:S(2)}, u32[]{:S(2)}) async-start(bf16[136,16,256]{2,0,1:T(8,128)(2,1)} %bitcast.30), calls=%async_computation | async-start | bytes 2228224 | tf_op jit(solution)/shard_map/all_to_all | solution.py:30
  17.0 0.6 multiply_reduce_fusion
  18.7 22.2 %all-to-all-done = bf16[136,16,256]{2,0,1:T(8,128)(2,1)S(1)} async-done(((bf16[136,16,256]{2,0,1:T(8,128)(2,1)}), bf16[136,16,256]{2,0,1:T(8,128)(2,1)S(1)}, u32[]{:S(2)}, u32[]{:S(2)}) %all-to-all-start) | async-done | bytes 1114144 | tf_op jit(solution)/shard_map/all_to_all | solution.py:30
  41.5 30.8 %while.1 = (s32[]{:T(128)}, bf16[2176,256]{1,0:T(8,128)(2,1)S(1)}, s32[16,2]{0,1:T(2,128)S(1)}, bf16[16,256,256]{2,1,0:T(8,128)(2,1)}, s32[]{:T(128)}) while((s32[]{:T(128)}, bf16[2176,256]{1,0:T(8,128)(2,1)S(1)}, s32[16,2]{0,1:T(2,128)S(1)}, bf16[16,256,256]{2,1,0:T(8,128)(2,1)}, s32[]{:T(128)}) %tuple.30), condition=%wide.while_cond, body=%wide.while_body.sunk | while | flops 2 | bytes 262757 | solution.py:35
  41.6 0.5 slice.63
  42.1 1.3 bitcast_dynamic-update-slice_fusion.2
  43.5 0.5 slice.63
  44.0 1.3 bitcast_dynamic-update-slice_fusion.2
  45.9 1.3 bitcast_dynamic-update-slice_fusion.2
  47.8 1.3 bitcast_dynamic-update-slice_fusion.2
  49.8 1.3 bitcast_dynamic-update-slice_fusion.2
  51.7 1.3 bitcast_dynamic-update-slice_fusion.2
  53.6 1.3 bitcast_dynamic-update-slice_fusion.2
  55.5 1.3 bitcast_dynamic-update-slice_fusion.2
  57.5 1.3 bitcast_dynamic-update-slice_fusion.2
  59.4 1.3 bitcast_dynamic-update-slice_fusion.2
  61.3 1.3 bitcast_dynamic-update-slice_fusion.2
  63.2 1.3 bitcast_dynamic-update-slice_fusion.2
  65.2 1.3 bitcast_dynamic-update-slice_fusion.2
  67.1 1.3 bitcast_dynamic-update-slice_fusion.2
  69.0 1.3 bitcast_dynamic-update-slice_fusion.2
  70.9 1.3 bitcast_dynamic-update-slice_fusion.2
  72.3 2.1 convolution_convert_fusion
  74.5 1.2 fusion.4
  75.8 92.7 %all-reduce.3.cloned.1.call-done = f32[32,32,32]{1,2,0:T(8,128)} async-done(((f32[32,32,32]{1,2,0:T(8,128)}), f32[32,32,32]{1,2,0:T(8,128)}) %all-reduce.3.cloned.1.call-update) | async-done | bytes 131088 | tf_op jit(solution)/shard_map/psum | solution.py:46
  168.4 1.4 fusion.17
  170.5 93.8 %custom-call.8 = f32[32,32,32]{2,1,0:T(8,128)S(1)} custom-call(f32[32,32,32]{2,1,0:T(8,128)S(1)} %fusion.2), custom_call_target="Cholesky" | custom-call | tf_op jit(solution)/shard_map/jit(cholesky)/cholesky | solution.py:56
  265.0 12.5 %custom-call.9 = f32[32,1,32,32]{0,2,3,1:T(8,128)S(1)} custom-call(f32[32,1,32,32]{0,3,2,1:T(8,128)S(1)} %get-tuple-element.25), custom_call_target="InvertDiagBlocksLowerTriangular" | custom-call | tf_op jit(solution)/shard_map/vmap(jit(_solve_triangular))/triangular_solve | solution.py:60
  277.5 0.6 copy.23
  278.1 1.3 copy.25
  279.4 1.6 fusion.1
  (59 shorter events, 10.8 us)
Async XLA Ops:
  7.2 11.1 %copy-start.2 = (s32[16]{0:T(128)S(1)}, s32[16]{0:T(128)}, u32[]{:S(2)}) copy-start(s32[16]{0:T(128)} %param.5) | copy-start | bytes 196
  7.2 11.2 %copy-start.1 = (s32[32]{0:T(128)S(1)}, s32[32]{0:T(128)}, u32[]{:S(2)}) copy-start(s32[32]{0:T(128)} %param.7) | copy-start | bytes 388
  7.2 11.3 %copy-start = (s32[32]{0:T(128)S(1)}, s32[32]{0:T(128)}, u32[]{:S(2)}) copy-start(s32[32]{0:T(128)} %param.6) | copy-start | bytes 388
  9.5 31.4 %all-to-all-start = ((bf16[136,16,256]{2,0,1:T(8,128)(2,1)}), bf16[136,16,256]{2,0,1:T(8,128)(2,1)S(1)}, u32[]{:S(2)}, u32[]{:S(2)}) async-start(bf16[136,16,256]{2,0,1:T(8,128)(2,1)} %bitcast.30), calls=%async_computation | async-start | bytes 2228224 | tf_op jit(solution)/shard_map/all_to_all | solution.py:30
  16.9 151.5 %all-reduce.3.cloned.1.call-start = ((), (), s32[]{:S(2)}) async-start(), calls=%async_computation.1 | async-start | bytes 1048576 | tf_op jit(solution)/shard_map/psum | solution.py:46
Sparse Core Ops, SparseCore 0:
  75.9 92.5 all-reduce.2
where the time goes:
time: 288 us
  waiting for transfers between devices  115 us (40%)
  other arithmetic  110 us (38%)
  local copies, waits for them, and re-layouts  35.5 us (12%)
  between operations  14.9 us (5%)
  starting transfers between devices  7.4 us (3%)
  matrix products  4.92 us (2%)
    another operation x4, other arithmetic, on_device(): lower_cholesky_matrix = jnp.linalg.cholesky(cross)  94 us
    psum x1, waiting for transfers between devices, on_device(): gram = lax.psum(local_gram, 'space')  92.7 us
    gather x48, local copies, waits for them, and re-layouts  30.8 us
    all_to_all x1, waiting for transfers between devices, on_device(): lax.all_to_all(arranged, 'space', split_axis=1, concat_axis=0, tiled=True)  22.2 us
    another operation x2, other arithmetic, solve_one(): return jax.scipy.linalg.solve_triangular(matrix, values, lower=True)  12.5 us
    all_to_all x1, starting transfers between devices, on_device(): lax.all_to_all(arranged, 'space', split_axis=1, concat_axis=0, tiled=True)  7.36 us
  transfers between devices with their start and end apart: 2, of which 2 were waited for; matrix products, arithmetic and copies ran while one was open for 0% of the time, Pallas kernels for 0%

commit v1 on v0

v1 whole, which is shorter than its diff:
```python
import math

import jax
import jax.numpy as jnp
from jax import lax
from jax.experimental import pallas as pl
from jax.experimental.pallas import tpu as pltpu
from jax.sharding import PartitionSpec as P

NB = 16
NWIN = 256
NFREQ = 32
NROW = 2 * NB
SPAN = NWIN + 16
LANES = 128
PER = LANES // NROW
GROUPS = NFREQ // PER


def make_table(bins):
    offsets = jnp.arange(NWIN, dtype=jnp.int32)
    window = 0.5 - 0.5 * jnp.cos(2.0 * math.pi * offsets.astype(jnp.float32) / NWIN)
    scaling = 1.0 / jnp.sqrt(jnp.sum(window * window))
    turns = bins[:, None] * offsets[None, :] % NWIN
    phases = 2.0 * math.pi * turns.astype(jnp.float32) / NWIN
    cos_rows = scaling * window[None, :] * jnp.cos(phases)
    sin_rows = -scaling * window[None, :] * jnp.sin(phases)
    return jnp.concatenate([cos_rows, sin_rows], axis=0)


def shift_kernel(shift_ref, table_ref, out_ref):
    rows = 2 * NFREQ
    wide = jnp.concatenate([table_ref[...], jnp.zeros((rows, LANES), jnp.float32)], axis=1)
    for b in range(NB):
        out_ref[b * rows : (b + 1) * rows, :] = pltpu.roll(wide, shift_ref[b], 1).astype(jnp.bfloat16)


def shift_tables(shifts, table):
    return pl.pallas_call(
        shift_kernel,
        out_shape=jax.ShapeDtypeStruct((NB * 2 * NFREQ, NWIN + LANES), jnp.bfloat16),
        in_specs=[
            pl.BlockSpec(memory_space=pltpu.SMEM),
            pl.BlockSpec(memory_space=pltpu.VMEM),
        ],
        out_specs=pl.BlockSpec(memory_space=pltpu.VMEM),
    )(shifts, table)


def spectra_kernel(first_ref, series_ref, table_ref, spectra_ref, gram_ref, centered_ref, rows_ref):
    times, points = series_ref.shape
    rows = 2 * NFREQ
    step = 128
    total = jnp.zeros((8, points), jnp.float32)
    for t in range(0, times, step):
        part = series_ref[t : t + step, :].astype(jnp.float32)
        total = total + jnp.sum(part.reshape(step // 8, 8, points), axis=0)
    mean = jnp.sum(total, axis=0, keepdims=True) * (1.0 / times)
    for t in range(0, times, step):
        part = series_ref[t : t + step, :].astype(jnp.float32)
        centered_ref[t : t + step, :] = (part - mean).astype(jnp.bfloat16)
    for b in range(NB):
        first = pl.multiple_of(first_ref[b], 16)
        window = centered_ref[pl.ds(first, SPAN), :]
        product = jnp.dot(
            table_ref[b * rows : (b + 1) * rows, :SPAN], window, preferred_element_type=jnp.float32
        )
        for c in range(0, points, LANES):
            rows_ref[c // LANES, pl.ds(b, NFREQ, stride=NROW), :] = product[:NFREQ, c : c + LANES]
            rows_ref[c // LANES, pl.ds(NB + b, NFREQ, stride=NROW), :] = product[NFREQ:, c : c + LANES]
    lane = lax.broadcasted_iota(jnp.int32, (NB, LANES), 1)
    segment = lax.broadcasted_iota(jnp.int32, (NROW, LANES), 1) // NROW
    left = lane % NROW < NB
    for g in range(GROUPS):
        stacked = jnp.concatenate(
            [rows_ref[c, g * LANES : (g + 1) * LANES, :] for c in range(points // LANES)], axis=1
        ).astype(jnp.bfloat16)
        spectra_ref[g * LANES : (g + 1) * LANES, :] = stacked
        gram = lax.dot_general(
            stacked, stacked, (((1,), (1,)), ((), ())), preferred_element_type=jnp.float32
        )
        own = gram[:NROW]
        for k in range(1, PER):
            own = jnp.where(segment == k, gram[k * NROW : (k + 1) * NROW], own)
        lower = own[NB:]
        swapped = jnp.where(left, pltpu.roll(lower, LANES - NB, 1), pltpu.roll(lower, NB, 1))
        gram_ref[pl.ds(g, NB, stride=GROUPS), :] = own[:NB] + jnp.where(left, swapped, -swapped)


def spectra_and_gram(first, series, tables):
    times, points = series.shape
    return pl.pallas_call(
        spectra_kernel,
        out_shape=(
            jax.ShapeDtypeStruct((NFREQ * NROW, points), jnp.bfloat16),
            jax.ShapeDtypeStruct((NB * GROUPS, LANES), jnp.float32),
        ),
        in_specs=[
            pl.BlockSpec(memory_space=pltpu.SMEM),
            pl.BlockSpec(memory_space=pltpu.VMEM),
            pl.BlockSpec(memory_space=pltpu.VMEM),
        ],
        out_specs=(
            pl.BlockSpec(memory_space=pltpu.VMEM),
            pl.BlockSpec(memory_space=pltpu.VMEM),
        ),
        scratch_shapes=[
            pltpu.VMEM((times, points), jnp.bfloat16),
            pltpu.VMEM((points // LANES, NFREQ * NROW, LANES), jnp.float32),
        ],
    )(first, series, tables)


def modes_kernel(scale, gram_ref, spectra_ref, count_ref, modes_ref, factor_ref, upper_ref, inverse_ref):
    lane = lax.broadcasted_iota(jnp.int32, (GROUPS, LANES), 1)
    column = lane % NROW
    base = lane - column
    left = column < NB
    count = count_ref[...]
    matrix = [None] * NROW
    for i in range(NB):
        row = gram_ref[i * GROUPS : (i + 1) * GROUPS, :] * scale
        matrix[i] = jnp.where(left, row, -row)
        matrix[NB + i] = jnp.where(left, pltpu.roll(row, LANES - NB, 1), pltpu.roll(row, NB, 1))
    sign = jnp.where(left, 1.0, -1.0)
    inverse = [jnp.where(column == i, sign, 0.0) for i in range(NROW)]

    def spread(row, i):
        return jnp.take_along_axis(row, base + i, axis=1)

    for k in range(NROW):
        root = lax.rsqrt(spread(matrix[k], k))
        upper = matrix[k] * root
        done = inverse[k] * root
        upper_ref[k * GROUPS : (k + 1) * GROUPS, :] = jnp.where(column >= k, upper, 0.0)
        inverse_ref[k * GROUPS : (k + 1) * GROUPS, :] = jnp.where(count > k % NB, done, 0.0)
        for i in range(k + 1, NROW):
            along = spread(upper, i)
            matrix[i] = matrix[i] - along * upper
            inverse[i] = inverse[i] - along * done
    for g in range(GROUPS):
        upper = upper_ref[pl.ds(g, NROW, stride=GROUPS), :]
        for k in range(PER):
            factor_ref[g * PER + k, :, :] = upper[:, k * NROW : (k + 1) * NROW]
    segment = lax.broadcasted_iota(jnp.int32, (NROW, LANES), 1) // NROW
    for g in range(GROUPS):
        weights = inverse_ref[pl.ds(g, NROW, stride=GROUPS), :]
        blocks = jnp.concatenate([jnp.where(segment == k, weights, 0.0) for k in range(PER)], axis=0)
        high = blocks.astype(jnp.bfloat16)
        low = (blocks - high.astype(jnp.float32)).astype(jnp.bfloat16)
        values = spectra_ref[g * LANES : (g + 1) * LANES, :]
        product = jnp.dot(high, values, preferred_element_type=jnp.float32) + jnp.dot(
            low, values, preferred_element_type=jnp.float32
        )
        modes_ref[g * LANES : (g + 1) * LANES, :] = product.astype(jnp.bfloat16)


def modes_and_factor(gram, spectra, counts, all_points):
    points = spectra.shape[1]

    def kernel(*refs):
        modes_kernel(1.0 / all_points, *refs)

    return pl.pallas_call(
        kernel,
        out_shape=(
            jax.ShapeDtypeStruct((NFREQ * NROW, points), jnp.bfloat16),
            jax.ShapeDtypeStruct((NFREQ, NROW, NROW), jnp.float32),
        ),
        in_specs=[pl.BlockSpec(memory_space=pltpu.VMEM)] * 3,
        out_specs=(
            pl.BlockSpec(memory_space=pltpu.VMEM),
            pl.BlockSpec(memory_space=pltpu.VMEM),
        ),
        scratch_shapes=[pltpu.VMEM((NROW * GROUPS, LANES), jnp.float32)] * 2,
    )(gram, spectra, counts)


def sum_over_space(partial, groups):
    if groups & (groups - 1):
        return lax.psum(partial, "space")
    bit = 1
    while bit < groups:
        moves = [bit]
        if bit == 2 and 2 * bit < groups:
            moves = [bit, 2 * bit, 3 * bit]
        parts = [
            lax.ppermute(partial, "space", [(i, i ^ move) for i in range(groups)]) for move in moves
        ]
        for part in parts:
            partial = partial + part
        bit *= 2 if len(moves) == 1 else 4
    return partial


def on_device(snapshots, starts, bins, mode_count):
    time_dev, all_points = snapshots.shape
    groups = lax.axis_size("space")
    points_dev = all_points // groups
    times = time_dev * groups
    arranged = jnp.swapaxes(snapshots.reshape(time_dev, groups, points_dev), 0, 1)
    series = lax.all_to_all(arranged, "space", split_axis=0, concat_axis=0, tiled=True)
    series = series.reshape(times, points_dev)
    first = jnp.minimum(starts // 16 * 16, times - SPAN)
    tables = shift_tables(starts - first, make_table(bins))
    spectra, partial = spectra_and_gram(first, series, tables)
    gram = sum_over_space(partial, groups)
    counts = jnp.repeat(mode_count.reshape(GROUPS, PER), NROW, axis=1)
    modes, factor = modes_and_factor(gram, spectra, counts, all_points)
    return (modes.reshape(NFREQ, NROW, points_dev), factor)


def solution(mesh):
    in_specs = (P("space", "parts"), P(), P(), P())
    out_specs = (P(None, None, ("parts", "space")), P("parts", None, None))
    return jax.shard_map(
        on_device, mesh=mesh, in_specs=in_specs, out_specs=out_specs, check_vma=False
    )
```

time: 288 us -> 64.5 us (0.22)
  other arithmetic: 110 us -> 3.58 us
  waiting for transfers between devices: 115 us -> 25.9 us
  local copies, waits for them, and re-layouts: 35.5 us -> 4.18 us
  between operations: 14.9 us -> 1.36 us
  Pallas kernels: 0 us -> 12.9 us
  starting transfers between devices: 7.4 us -> 16.2 us
  matrix products: 4.92 us -> 0 us
    another operation x7 -> x0, other arithmetic: 107 us -> none  [the longest x4 94 us: on_device(): lower_cholesky_matrix = jnp.linalg.cholesky(cross)]
    psum x1 -> x0, waiting for transfers between devices: 92.7 us -> none  [on_device(): gram = lax.psum(local_gram, 'space')]
    gather x48 -> x0, local copies, waits for them, and re-layouts: 30.8 us -> none
    pallas_call x0 -> x3, Pallas kernels: none -> 12.9 us  [the longest x1 6.82 us: modes_and_factor(): pl.pallas_call(kernel, out_shape=(jax.ShapeDtypeStruct((NFREQ * NROW, poi...]
    ppermute x0 -> x5, starting transfers between devices: none -> 8.7 us  [sum_over_space(): lax.ppermute(partial, 'space', [(i, i ^ move) for i in range(groups)])]
    ppermute x0 -> x5, waiting for transfers between devices: none -> 6.76 us  [sum_over_space(): lax.ppermute(partial, 'space', [(i, i ^ move) for i in range(groups)])]
    dot_general x2 -> x0, matrix products: 3.29 us -> none  [the longest x1 2.07 us: on_device(): jnp.einsum('vx,oxy->voy', fourier_table, welch_windows, preferred_element...]
    all_to_all x1, waiting for transfers between devices: 22.2 us -> 19.1 us  [on_device(): lax.all_to_all(arranged, 'space', split_axis=0, concat_axis=0, tiled=True)]
  transfers between devices with their start and end apart: 2 -> 6, of which waited for: 2 -> 5; matrix products, arithmetic and copies ran while one was open for 0% -> 5% of each run, Pallas kernels for 0% -> 3%
where the time goes in v1:
time: 64.5 us; the launch traced here: 64.2 us
  waiting for transfers between devices  25.9 us (40%)
  starting transfers between devices  16.2 us (25%)
  Pallas kernels  12.9 us (20%)
  local copies, waits for them, and re-layouts  4.18 us (6%)
  other arithmetic  3.58 us (6%)
  between operations  1.36 us (2%)
    all_to_all x1, waiting for transfers between devices, on_device(): lax.all_to_all(arranged, 'space', split_axis=0, concat_axis=0, tiled=True)  19.1 us
    ppermute x5, starting transfers between devices, sum_over_space(): lax.ppermute(partial, 'space', [(i, i ^ move) for i in range(groups)])  8.7 us
    all_to_all x1, starting transfers between devices, on_device(): lax.all_to_all(arranged, 'space', split_axis=0, concat_axis=0, tiled=True)  7.49 us
    pallas_call x1, Pallas kernels, modes_and_factor(): pl.pallas_call(kernel, out_shape=(jax.ShapeDtypeStruct((NFREQ * NROW, poi...  6.82 us
    ppermute x5, waiting for transfers between devices, sum_over_space(): lax.ppermute(partial, 'space', [(i, i ^ move) for i in range(groups)])  6.76 us
    pallas_call x1, Pallas kernels, spectra_and_gram(): pl.pallas_call(spectra_kernel, out_shape=(jax.ShapeDtypeStruct((NFREQ * N...  4.04 us
    reshape x1, local copies, waits for them, and re-layouts, on_device(): snapshots.reshape(time_dev, groups, points_dev)  2.33 us
    pallas_call x1, Pallas kernels, shift_tables(): pl.pallas_call(shift_kernel, out_shape=jax.ShapeDtypeStruct((NB * 2 * NFR...  2.09 us
  transfers between devices with their start and end apart: 6, of which 5 were waited for; matrix products, arithmetic and copies ran while one was open for 5% of the time, Pallas kernels for 3%

profile of v1, /device:TPU:0, one launch (start us, length us, event | category | flops | bytes accessed | tf_op | source)
XLA Modules:
  0.0 64.2 jit_solution(1513968702542166084)
XLA Ops:
  0.6 2.3 %copy.10 = bf16[17,16,8,256]{3,2,0,1:T(8,128)(2,1)} copy(bf16[17,16,8,256]{3,2,1,0:T(8,128)(2,1)} %bitcast.10) | data formatting | bytes 2228224 | tf_op jit(solution)/shard_map/reshape | solution.py:201
  3.0 0.0 copy-start.1
  3.0 0.0 copy-start.3
  3.0 7.5 %all-to-all-start = ((bf16[16,136,256]{2,1,0:T(8,128)(2,1)}), bf16[16,136,256]{2,1,0:T(8,128)(2,1)S(1)}, u32[]{:S(2)}, u32[]{:S(2)}) async-start(bf16[16,136,256]{2,1,0:T(8,128)(2,1)} %bitcast.8), calls=%async_computation | async-start | bytes 2228224 | tf_op jit(solution)/shard_map/all_to_all | solution.py:202
  10.5 0.6 %multiply_reduce_fusion = f32[]{:T(128)} fusion(), kind=kLoop, calls=%fused_computation.18 | loop fusion | flops 1535 | bytes 4 | tf_op jit(solution)/shard_map/reduce_sum | solution.py:23
  11.8 0.0 copy-done.1
  11.9 0.2 cosine_multiply_fusion
  12.1 0.6 pad_maximum_fusion.table_ref
  12.7 0.0 copy-done.3
  12.7 0.5 fusion.6
  13.2 2.1 %shard_map.59.table_ref = bf16[1024,384]{1,0:T(8,128)(2,1)} custom-call(s32[16]{0:T(128)} %get-tuple-element.10.shift_ref, f32[64,256]{1,0:T(8,128)} %pad_maximum_fusion.table_ref), custom_call_target="tpu_custom_call" | custom-call | tf_op jit(solution)/shard_map/pallas_call | solution.py:39
  15.3 19.1 %all-to-all-done = bf16[16,136,256]{2,1,0:T(8,128)(2,1)S(1)} async-done(((bf16[16,136,256]{2,1,0:T(8,128)(2,1)}), bf16[16,136,256]{2,1,0:T(8,128)(2,1)S(1)}, u32[]{:S(2)}, u32[]{:S(2)}) %all-to-all-start) | async-done | bytes 1114144 | tf_op jit(solution)/shard_map/all_to_all | solution.py:202
  34.5 0.0 copy-start
  34.5 1.0 %copy-done = bf16[16,136,256]{2,1,0:T(8,128)(2,1)} copy-done((bf16[16,136,256]{2,1,0:T(8,128)(2,1)}, bf16[16,136,256]{2,1,0:T(8,128)(2,1)S(1)}, u32[]{:S(2)}) %copy-start) | copy-done | bytes 1114136
  35.5 4.0 %shard_map.60 = (bf16[1024,256]{1,0:T(8,128)(2,1)}, f32[128,128]{1,0:T(8,128)}) custom-call(s32[16]{0:T(128)} %get-tuple-element.11.first_ref, bf16[2176,256]{1,0:T(8,128)(2,1)} %bitcast.9, bf16[1024,384]{1,0:T(8,128)(2,1)} %shard_map.59.table_ref), custom_call_target="tpu_custom_call" | custom-call | tf_op jit(solution)/shard_map/pallas_call | solution.py:92
  39.5 0.7 %collective-permute-start = (f32[128,128]{1,0:T(8,128)}, f32[128,128]{1,0:T(8,128)S(1)}, u32[]{:S(2)}, u32[]{:S(2)}) collective-permute-start(f32[128,128]{1,0:T(8,128)} %get-tuple-element.6), channel_id=1, source_target_pairs={{0,1},{1,0},{2,3},{3,2},{4,5},{5,4},{6,7},{7,6},{8,9},{9,8},{10,11... | collective-permute-start | bytes 196616 | tf_op jit(solution)/shard_map/ppermute | solution.py:188
  40.3 1.1 %collective-permute-done = f32[128,128]{1,0:T(8,128)S(1)} collective-permute-done((f32[128,128]{1,0:T(8,128)}, f32[128,128]{1,0:T(8,128)S(1)}, u32[]{:S(2)}, u32[]{:S(2)}) %collective-permute-start) | collective-permute-done | bytes 65568 | tf_op jit(solution)/shard_map/ppermute | solution.py:188
  41.4 0.9 %add.23 = f32[128,128]{1,0:T(8,128)S(1)} add(f32[128,128]{1,0:T(8,128)} %get-tuple-element.6, f32[128,128]{1,0:T(8,128)S(1)} %collective-permute-done) | non-fusion elementwise | flops 16384 | bytes 196608 | tf_op jit(solution)/shard_map/add | solution.py:191
  42.2 4.7 %collective-permute-start.3 = (f32[128,128]{1,0:T(8,128)S(1)}, f32[128,128]{1,0:T(8,128)S(1)}, u32[]{:S(2)}, u32[]{:S(2)}) collective-permute-start(f32[128,128]{1,0:T(8,128)S(1)} %add.23), channel_id=1, source_target_pairs={{0,6},{1,7},{2,4},{3,5},{4,2},{5,3},{6,0},{7,1},{8,14},{9,15},{10,... | collective-permute-start | bytes 196616 | tf_op jit(solution)/shard_map/ppermute | solution.py:188
  46.9 0.0 collective-permute-start.2
  46.9 0.6 collective-permute-start.1
  47.5 2.0 %collective-permute-done.3 = f32[128,128]{1,0:T(8,128)S(1)} collective-permute-done((f32[128,128]{1,0:T(8,128)S(1)}, f32[128,128]{1,0:T(8,128)S(1)}, u32[]{:S(2)}, u32[]{:S(2)}) %collective-permute-start.3) | collective-permute-done | bytes 65568 | tf_op jit(solution)/shard_map/ppermute | solution.py:188
  49.5 1.7 %collective-permute-done.2 = f32[128,128]{1,0:T(8,128)S(1)} collective-permute-done((f32[128,128]{1,0:T(8,128)S(1)}, f32[128,128]{1,0:T(8,128)S(1)}, u32[]{:S(2)}, u32[]{:S(2)}) %collective-permute-start.2) | collective-permute-done | bytes 65568 | tf_op jit(solution)/shard_map/ppermute | solution.py:188
  51.2 0.0 collective-permute-done.1
  51.2 2.6 %collective-permute-start.4 = (f32[128,128]{1,0:T(8,128)S(1)}, f32[128,128]{1,0:T(8,128)S(1)}, u32[]{:S(2)}, u32[]{:S(2)}) collective-permute-start(f32[128,128]{1,0:T(8,128)S(1)} %add_add_fusion), channel_id=1, source_target_pairs={{0,8},{1,9},{2,10},{3,11},{4,12},{5,13},{6,14},{7,15},{8,0},{9,1},... | collective-permute-start | bytes 196616 | tf_op jit(solution)/shard_map/ppermute | solution.py:188
  53.8 0.0 copy-done.2
  53.8 0.1 reshape.36
  53.9 0.1 broadcast_in_dim.2
  54.0 0.7 %reshape.37.refs_2_ = s32[8,128]{1,0:T(8,128)} reshape(s32[8,4,32]{2,1,0:T(4,128)S(1)} %broadcast_in_dim.2) | data formatting | bytes 8192 | tf_op jit(solution)/shard_map/reshape | solution.py:208
  54.7 2.0 %collective-permute-done.4 = f32[128,128]{1,0:T(8,128)S(1)} collective-permute-done((f32[128,128]{1,0:T(8,128)S(1)}, f32[128,128]{1,0:T(8,128)S(1)}, u32[]{:S(2)}, u32[]{:S(2)}) %collective-permute-start.4) | collective-permute-done | bytes 65568 | tf_op jit(solution)/shard_map/ppermute | solution.py:188
  56.7 0.6 add.27.refs_0_
  57.3 6.8 %shard_map.61 = (bf16[1024,256]{1,0:T(8,128)(2,1)}, f32[32,32,32]{2,1,0:T(8,128)}) custom-call(f32[128,128]{1,0:T(8,128)} %add.27.refs_0_, bf16[1024,256]{1,0:T(8,128)(2,1)} %get-tuple-element.7.refs_1_, s32[8,128]{1,0:T(8,128)} %reshape.37.refs_2_), custom_call_target="tpu_custom_call" | custom-call | tf_op jit(solution)/shard_map/pallas_call | solution.py:164
  (3 shorter events, 0.1 us)
Async XLA Ops:
  3.0 8.9 %copy-start.1 = (s32[32]{0:T(128)S(1)}, s32[32]{0:T(128)}, u32[]{:S(2)}) copy-start(s32[32]{0:T(128)} %param.6) | copy-start | bytes 388
  3.0 9.8 %copy-start.3 = (s32[16]{0:T(128)S(1)}, s32[16]{0:T(128)}, u32[]{:S(2)}) copy-start(s32[16]{0:T(128)} %param.5) | copy-start | bytes 196
  3.0 31.5 %all-to-all-start = ((bf16[16,136,256]{2,1,0:T(8,128)(2,1)}), bf16[16,136,256]{2,1,0:T(8,128)(2,1)S(1)}, u32[]{:S(2)}, u32[]{:S(2)}) async-start(bf16[16,136,256]{2,1,0:T(8,128)(2,1)} %bitcast.8), calls=%async_computation | async-start | bytes 2228224 | tf_op jit(solution)/shard_map/all_to_all | solution.py:202
  34.5 1.0 %copy-start = (bf16[16,136,256]{2,1,0:T(8,128)(2,1)}, bf16[16,136,256]{2,1,0:T(8,128)(2,1)S(1)}, u32[]{:S(2)}) copy-start(bf16[16,136,256]{2,1,0:T(8,128)(2,1)S(1)} %all-to-all-done) | copy-start | bytes 3342340
  35.5 18.4 %copy-start.2 = (s32[32]{0:T(128)S(1)}, s32[32]{0:T(128)}, u32[]{:S(2)}) copy-start(s32[32]{0:T(128)} %param.7) | copy-start | bytes 388
  39.5 1.9 %collective-permute-start = (f32[128,128]{1,0:T(8,128)}, f32[128,128]{1,0:T(8,128)S(1)}, u32[]{:S(2)}, u32[]{:S(2)}) collective-permute-start(f32[128,128]{1,0:T(8,128)} %get-tuple-element.6), channel_id=1, source_target_pairs={{0,1},{1,0},{2,3},{3,2},{4,5},{5,4},{6,7},{7,6},{8,9},{9,8},{10,11... | collective-permute-start | bytes 196616 | tf_op jit(solution)/shard_map/ppermute | solution.py:188
  42.2 7.3 %collective-permute-start.3 = (f32[128,128]{1,0:T(8,128)S(1)}, f32[128,128]{1,0:T(8,128)S(1)}, u32[]{:S(2)}, u32[]{:S(2)}) collective-permute-start(f32[128,128]{1,0:T(8,128)S(1)} %add.23), channel_id=1, source_target_pairs={{0,6},{1,7},{2,4},{3,5},{4,2},{5,3},{6,0},{7,1},{8,14},{9,15},{10,... | collective-permute-start | bytes 196616 | tf_op jit(solution)/shard_map/ppermute | solution.py:188
  46.9 4.3 %collective-permute-start.2 = (f32[128,128]{1,0:T(8,128)S(1)}, f32[128,128]{1,0:T(8,128)S(1)}, u32[]{:S(2)}, u32[]{:S(2)}) collective-permute-start(f32[128,128]{1,0:T(8,128)S(1)} %add.23), channel_id=1, source_target_pairs={{0,4},{1,5},{2,6},{3,7},{4,0},{5,1},{6,2},{7,3},{8,12},{9,13},{10,... | collective-permute-start | bytes 196616 | tf_op jit(solution)/shard_map/ppermute | solution.py:188
  46.9 4.3 %collective-permute-start.1 = (f32[128,128]{1,0:T(8,128)S(1)}, f32[128,128]{1,0:T(8,128)S(1)}, u32[]{:S(2)}, u32[]{:S(2)}) collective-permute-start(f32[128,128]{1,0:T(8,128)S(1)} %add.23), channel_id=1, source_target_pairs={{0,2},{1,3},{2,0},{3,1},{4,6},{5,7},{6,4},{7,5},{8,10},{9,11},{10,... | collective-permute-start | bytes 196616 | tf_op jit(solution)/shard_map/ppermute | solution.py:188
  51.2 5.5 %collective-permute-start.4 = (f32[128,128]{1,0:T(8,128)S(1)}, f32[128,128]{1,0:T(8,128)S(1)}, u32[]{:S(2)}, u32[]{:S(2)}) collective-permute-start(f32[128,128]{1,0:T(8,128)S(1)} %add_add_fusion), channel_id=1, source_target_pairs={{0,8},{1,9},{2,10},{3,11},{4,12},{5,13},{6,14},{7,15},{8,0},{9,1},... | collective-permute-start | bytes 196616 | tf_op jit(solution)/shard_map/ppermute | solution.py:188

commit v2 on v1

--- a/solution.py
+++ b/solution.py
@@ -15,6 +15,9 @@
 LANES = 128
 PER = LANES // NROW
 GROUPS = NFREQ // PER
+HALF = NB // 2
+BLOCK = 4
+VMEM = pltpu.CompilerParams(vmem_limit_bytes=16 * 1024 * 1024)
 
 
 def make_table(bins):
@@ -44,6 +47,7 @@
             pl.BlockSpec(memory_space=pltpu.VMEM),
         ],
         out_specs=pl.BlockSpec(memory_space=pltpu.VMEM),
+        compiler_params=VMEM,
     )(shifts, table)
 
 
@@ -68,7 +72,7 @@
         for c in range(0, points, LANES):
             rows_ref[c // LANES, pl.ds(b, NFREQ, stride=NROW), :] = product[:NFREQ, c : c + LANES]
             rows_ref[c // LANES, pl.ds(NB + b, NFREQ, stride=NROW), :] = product[NFREQ:, c : c + LANES]
-    lane = lax.broadcasted_iota(jnp.int32, (NB, LANES), 1)
+    lane = lax.broadcasted_iota(jnp.int32, (HALF, LANES), 1)
     segment = lax.broadcasted_iota(jnp.int32, (NROW, LANES), 1) // NROW
     left = lane % NROW < NB
     for g in range(GROUPS):
@@ -82,9 +86,11 @@
         own = gram[:NROW]
         for k in range(1, PER):
             own = jnp.where(segment == k, gram[k * NROW : (k + 1) * NROW], own)
-        lower = own[NB:]
-        swapped = jnp.where(left, pltpu.roll(lower, LANES - NB, 1), pltpu.roll(lower, NB, 1))
-        gram_ref[pl.ds(g, NB, stride=GROUPS), :] = own[:NB] + jnp.where(left, swapped, -swapped)
+        upper, lower = own[:NB], own[NB:]
+        mixed = (upper - lower) + pltpu.roll(upper + lower, LANES - NB, 1)
+        gram_ref[pl.ds(g, HALF, stride=GROUPS), :] = jnp.where(
+            left, mixed[:HALF], pltpu.roll(mixed[HALF:], NB, 1)
+        )
 
 
 def spectra_and_gram(first, series, tables):
@@ -93,7 +99,7 @@
         spectra_kernel,
         out_shape=(
             jax.ShapeDtypeStruct((NFREQ * NROW, points), jnp.bfloat16),
-            jax.ShapeDtypeStruct((NB * GROUPS, LANES), jnp.float32),
+            jax.ShapeDtypeStruct((HALF * GROUPS, LANES), jnp.float32),
         ),
         in_specs=[
             pl.BlockSpec(memory_space=pltpu.SMEM),
@@ -108,36 +114,73 @@
             pltpu.VMEM((times, points), jnp.bfloat16),
             pltpu.VMEM((points // LANES, NFREQ * NROW, LANES), jnp.float32),
         ],
+        compiler_params=VMEM,
     )(first, series, tables)
 
 
-def modes_kernel(scale, gram_ref, spectra_ref, count_ref, modes_ref, factor_ref, upper_ref, inverse_ref):
+def unpack(packed):
+    lane = lax.broadcasted_iota(jnp.int32, (GROUPS, LANES), 1)
+    left = lane % NROW < NB
+    rows = packed + [pltpu.roll(row, LANES - NB, 1) for row in packed]
+    turned = list(rows)
+    bit = 1
+    while bit < NB:
+        high = (lane & bit) != 0
+        turned = [
+            jnp.where(high, turned[i], pltpu.roll(turned[i - bit], LANES - bit, 1))
+            if i & bit
+            else jnp.where(high, pltpu.roll(turned[i + bit], bit, 1), turned[i])
+            for i in range(NB)
+        ]
+        bit *= 2
+    sums = [rows[i] + turned[i] for i in range(NB)]
+    minus = [turned[i] - rows[i] for i in range(NB)]
+    upper = [jnp.where(left, sums[i], pltpu.roll(minus[i], NB, 1)) for i in range(NB)]
+    return upper + [pltpu.roll(row, NB, 1) for row in sums]
+
+
+def modes_kernel(
+    scale, gram_ref, other_ref, spectra_ref, count_ref, modes_ref, factor_ref, upper_ref, inverse_ref
+):
     lane = lax.broadcasted_iota(jnp.int32, (GROUPS, LANES), 1)
     column = lane % NROW
     base = lane - column
-    left = column < NB
     count = count_ref[...]
-    matrix = [None] * NROW
-    for i in range(NB):
-        row = gram_ref[i * GROUPS : (i + 1) * GROUPS, :] * scale
-        matrix[i] = jnp.where(left, row, -row)
-        matrix[NB + i] = jnp.where(left, pltpu.roll(row, LANES - NB, 1), pltpu.roll(row, NB, 1))
-    sign = jnp.where(left, 1.0, -1.0)
+    matrix = unpack(
+        [
+            (gram_ref[r * GROUPS : (r + 1) * GROUPS, :] + other_ref[r * GROUPS : (r + 1) * GROUPS, :])
+            * (0.5 * scale)
+            for r in range(HALF)
+        ]
+    )
+    sign = jnp.where(column < NB, 1.0, -1.0)
     inverse = [jnp.where(column == i, sign, 0.0) for i in range(NROW)]
 
     def spread(row, i):
         return jnp.take_along_axis(row, base + i, axis=1)
 
-    for k in range(NROW):
-        root = lax.rsqrt(spread(matrix[k], k))
-        upper = matrix[k] * root
-        done = inverse[k] * root
-        upper_ref[k * GROUPS : (k + 1) * GROUPS, :] = jnp.where(column >= k, upper, 0.0)
-        inverse_ref[k * GROUPS : (k + 1) * GROUPS, :] = jnp.where(count > k % NB, done, 0.0)
-        for i in range(k + 1, NROW):
-            along = spread(upper, i)
-            matrix[i] = matrix[i] - along * upper
-            inverse[i] = inverse[i] - along * done
+    for first in range(0, NROW, BLOCK):
+        block = range(first, first + BLOCK)
+        along = {(k, i): spread(matrix[k], i) for k in block for i in range(k, NROW)}
+        scaled, solved = {}, {}
+        for k in block:
+            root = lax.rsqrt(along[k, k])
+            upper_ref[k * GROUPS : (k + 1) * GROUPS, :] = jnp.where(column >= k, matrix[k] * root, 0.0)
+            inverse_ref[k * GROUPS : (k + 1) * GROUPS, :] = jnp.where(count > k % NB, inverse[k] * root, 0.0)
+            over = root * root
+            scaled[k] = matrix[k] * over
+            solved[k] = inverse[k] * over
+            for p in range(k + 1, first + BLOCK):
+                entry = along[k, p]
+                matrix[p] = matrix[p] - entry * scaled[k]
+                inverse[p] = inverse[p] - entry * solved[k]
+                ratio = entry * over
+                for i in range(p, NROW):
+                    along[p, i] = along[p, i] - ratio * along[k, i]
+        for i in range(first + BLOCK, NROW):
+            for k in block:
+                matrix[i] = matrix[i] - along[k, i] * scaled[k]
+                inverse[i] = inverse[i] - along[k, i] * solved[k]
     for g in range(GROUPS):
         upper = upper_ref[pl.ds(g, NROW, stride=GROUPS), :]
         for k in range(PER):
@@ -155,7 +198,7 @@
         modes_ref[g * LANES : (g + 1) * LANES, :] = product.astype(jnp.bfloat16)
 
 
-def modes_and_factor(gram, spectra, counts, all_points):
+def modes_and_factor(gram, other, spectra, counts, all_points):
     points = spectra.shape[1]
 
     def kernel(*refs):
@@ -167,30 +210,36 @@
             jax.ShapeDtypeStruct((NFREQ * NROW, points), jnp.bfloat16),
             jax.ShapeDtypeStruct((NFREQ, NROW, NROW), jnp.float32),
         ),
-        in_specs=[pl.BlockSpec(memory_space=pltpu.VMEM)] * 3,
+        in_specs=[pl.BlockSpec(memory_space=pltpu.VMEM)] * 4,
         out_specs=(
             pl.BlockSpec(memory_space=pltpu.VMEM),
             pl.BlockSpec(memory_space=pltpu.VMEM),
         ),
         scratch_shapes=[pltpu.VMEM((NROW * GROUPS, LANES), jnp.float32)] * 2,
-    )(gram, spectra, counts)
+        compiler_params=VMEM,
+    )(gram, other, spectra, counts)
 
 
 def sum_over_space(partial, groups):
-    if groups & (groups - 1):
-        return lax.psum(partial, "space")
-    bit = 1
+    if groups & (groups - 1) or groups == 1:
+        return lax.psum(partial, "space"), jnp.zeros_like(partial)
+    bit, rounds = 1, []
     while bit < groups:
-        moves = [bit]
-        if bit == 2 and 2 * bit < groups:
-            moves = [bit, 2 * bit, 3 * bit]
+        if bit == 2 and 4 * bit < groups:
+            rounds.append([bit, 2 * bit, 3 * bit])
+            bit *= 4
+        else:
+            rounds.append([bit])
+            bit *= 2
+    for moves in rounds:
         parts = [
             lax.ppermute(partial, "space", [(i, i ^ move) for i in range(groups)]) for move in moves
         ]
-        for part in parts:
-            partial = partial + part
-        bit *= 2 if len(moves) == 1 else 4
-    return partial
+        left, right = partial, parts[0]
+        if len(moves) == 3:
+            left, right = partial + parts[0], parts[1] + parts[2]
+        partial = left + right
+    return left, right
 
 
 def on_device(snapshots, starts, bins, mode_count):
@@ -204,9 +253,9 @@
     first = jnp.minimum(starts // 16 * 16, times - SPAN)
     tables = shift_tables(starts - first, make_table(bins))
     spectra, partial = spectra_and_gram(first, series, tables)
-    gram = sum_over_space(partial, groups)
+    gram, other = sum_over_space(partial, groups)
     counts = jnp.repeat(mode_count.reshape(GROUPS, PER), NROW, axis=1)
-    modes, factor = modes_and_factor(gram, spectra, counts, all_points)
+    modes, factor = modes_and_factor(gram, other, spectra, counts, all_points)
     return (modes.reshape(NFREQ, NROW, points_dev), factor)
 
 

time: 64.5 us -> 55.5 us (0.86)
  Pallas kernels: 12.9 us -> 6.36 us
  waiting for transfers between devices: 25.9 us -> 28.8 us
  other arithmetic: 3.58 us -> 0.95 us
  local copies, waits for them, and re-layouts: 4.18 us -> 2.56 us
  starting transfers between devices: 16.2 us -> 15.2 us
    pallas_call x1, Pallas kernels: 6.82 us -> 2.99 us  [modes_and_factor(): pl.pallas_call(kernel, out_shape=(jax.ShapeDtypeStruct((NFREQ * NROW, poi...]
    all_to_all x1, waiting for transfers between devices: 19.1 us -> 21.5 us  [on_device(): lax.all_to_all(arranged, 'space', split_axis=0, concat_axis=0, tiled=True)]
    pallas_call x1, Pallas kernels: 4.04 us -> 2.52 us  [spectra_and_gram(): pl.pallas_call(spectra_kernel, out_shape=(jax.ShapeDtypeStruct((NFREQ * N...]
    add x3 -> x2, other arithmetic: 1.5 us -> 0.01 us  [sum_over_space(): partial = left + right]
    pallas_call x1, Pallas kernels: 2.09 us -> 0.85 us  [shift_tables(): pl.pallas_call(shift_kernel, out_shape=jax.ShapeDtypeStruct((NB * 2 * NFR...]
    ppermute x5, starting transfers between devices: 8.7 us -> 7.68 us  [sum_over_space(): lax.ppermute(partial, 'space', [(i, i ^ move) for i in range(groups)])]
    unnamed x8 -> x6, local copies, waits for them, and re-layouts: 1.02 us -> 0.01 us
  transfers between devices with their start and end apart: 6 -> 6, of which waited for: 5 -> 6; matrix products, arithmetic and copies ran while one was open for 5% -> 2% of each run, Pallas kernels for 3% -> 2%
where the time goes in v2:
time: 55.5 us; the launch traced here: 55.2 us
  waiting for transfers between devices  28.8 us (52%)
  starting transfers between devices  15.2 us (27%)
  Pallas kernels  6.36 us (11%)
  local copies, waits for them, and re-layouts  2.56 us (5%)
  between operations  1.39 us (3%)
  other arithmetic  0.95 us (2%)
    all_to_all x1, waiting for transfers between devices, on_device(): lax.all_to_all(arranged, 'space', split_axis=0, concat_axis=0, tiled=True)  21.5 us
    ppermute x5, starting transfers between devices, sum_over_space(): lax.ppermute(partial, 'space', [(i, i ^ move) for i in range(groups)])  7.68 us
    all_to_all x1, starting transfers between devices, on_device(): lax.all_to_all(arranged, 'space', split_axis=0, concat_axis=0, tiled=True)  7.49 us
    ppermute x5, waiting for transfers between devices, sum_over_space(): lax.ppermute(partial, 'space', [(i, i ^ move) for i in range(groups)])  7.29 us
    pallas_call x1, Pallas kernels, modes_and_factor(): pl.pallas_call(kernel, out_shape=(jax.ShapeDtypeStruct((NFREQ * NROW, poi...  2.99 us
    pallas_call x1, Pallas kernels, spectra_and_gram(): pl.pallas_call(spectra_kernel, out_shape=(jax.ShapeDtypeStruct((NFREQ * N...  2.52 us
    reshape x1, local copies, waits for them, and re-layouts, on_device(): snapshots.reshape(time_dev, groups, points_dev)  2.31 us
  transfers between devices with their start and end apart: 6, of which 6 were waited for; matrix products, arithmetic and copies ran while one was open for 2% of the time, Pallas kernels for 2%

profile of v2, /device:TPU:0, one launch (start us, length us, event | category | flops | bytes accessed | tf_op | source)
XLA Modules:
  0.0 55.2 jit_solution(12868146464160645078)
XLA Ops:
  0.6 2.3 %copy.10 = bf16[17,16,8,256]{3,2,0,1:T(8,128)(2,1)} copy(bf16[17,16,8,256]{3,2,1,0:T(8,128)(2,1)} %bitcast.10) | data formatting | bytes 2228224 | tf_op jit(solution)/shard_map/reshape | solution.py:250
  2.9 0.0 copy-start
  2.9 0.0 copy-start.2
  2.9 7.5 %all-to-all-start = ((bf16[16,136,256]{2,1,0:T(8,128)(2,1)}), bf16[16,136,256]{2,1,0:T(8,128)(2,1)S(1)}, u32[]{:S(2)}, u32[]{:S(2)}) async-start(bf16[16,136,256]{2,1,0:T(8,128)(2,1)} %bitcast.8), calls=%async_computation | async-start | bytes 2228224 | tf_op jit(solution)/shard_map/all_to_all | solution.py:251
  10.4 0.6 %multiply_reduce_fusion = f32[]{:T(128)} fusion(), kind=kLoop, calls=%fused_computation.18 | loop fusion | flops 1535 | bytes 4 | tf_op jit(solution)/shard_map/reduce_sum | solution.py:26
  11.8 0.0 copy-done
  11.8 0.2 cosine_multiply_fusion
  12.1 0.0 copy-done.2
  12.1 0.9 %shard_map.59.table_ref = bf16[1024,384]{1,0:T(8,128)(2,1)S(1)} custom-call(s32[16]{0:T(128)S(1)} %get-tuple-element.10.shift_ref, f32[64,256]{1,0:T(8,128)S(1)} %pad_maximum_fusion.table_ref), custom_call_target="tpu_custom_call" | custom-call | tf_op jit(solution)/shard_map/pallas_call | solution.py:42
  13.0 0.0 copy-start.1
  13.0 21.5 %all-to-all-done = bf16[16,136,256]{2,1,0:T(8,128)(2,1)S(1)} async-done(((bf16[16,136,256]{2,1,0:T(8,128)(2,1)}), bf16[16,136,256]{2,1,0:T(8,128)(2,1)S(1)}, u32[]{:S(2)}, u32[]{:S(2)}) %all-to-all-start) | async-done | bytes 1114144 | tf_op jit(solution)/shard_map/all_to_all | solution.py:251
  34.5 2.5 %shard_map.60 = (bf16[1024,256]{1,0:T(8,128)(2,1)S(1)}, f32[64,128]{1,0:T(8,128)S(1)}) custom-call(s32[16]{0:T(128)S(1)} %get-tuple-element.11.first_ref, bf16[2176,256]{1,0:T(8,128)(2,1)S(1)} %bitcast.9, bf16[1024,384]{1,0:T(8,128)(2,1)S(1)} %shard_map.59.table_ref), custom_call_target="tpu_custom_call" | custom-call | tf_op jit(solution)/shard_map/pallas_call | solution.py:98
  37.0 0.8 %collective-permute-start = (f32[64,128]{1,0:T(8,128)S(1)}, f32[64,128]{1,0:T(8,128)S(1)}, u32[]{:S(2)}, u32[]{:S(2)}) collective-permute-start(f32[64,128]{1,0:T(8,128)S(1)} %get-tuple-element.6), channel_id=1, source_target_pairs={{0,1},{1,0},{2,3},{3,2},{4,5},{5,4},{6,7},{7,6},{8,9},{9,8},{10,11... | collective-permute-start | bytes 98312 | tf_op jit(solution)/shard_map/ppermute | solution.py:236
  37.8 0.9 %collective-permute-done = f32[64,128]{1,0:T(8,128)S(1)} collective-permute-done((f32[64,128]{1,0:T(8,128)S(1)}, f32[64,128]{1,0:T(8,128)S(1)}, u32[]{:S(2)}, u32[]{:S(2)}) %collective-permute-start) | collective-permute-done | bytes 32800 | tf_op jit(solution)/shard_map/ppermute | solution.py:236
  38.6 3.5 %collective-permute-start.2 = (f32[64,128]{1,0:T(8,128)S(1)}, f32[64,128]{1,0:T(8,128)S(1)}, u32[]{:S(2)}, u32[]{:S(2)}) collective-permute-start(f32[64,128]{1,0:T(8,128)S(1)} %add.20), channel_id=1, source_target_pairs={{0,4},{1,5},{2,6},{3,7},{4,0},{5,1},{6,2},{7,3},{8,12},{9,13},{10,... | collective-permute-start | bytes 98312 | tf_op jit(solution)/shard_map/ppermute | solution.py:236
  42.2 1.1 %collective-permute-start.3 = (f32[64,128]{1,0:T(8,128)S(1)}, f32[64,128]{1,0:T(8,128)S(1)}, u32[]{:S(2)}, u32[]{:S(2)}) collective-permute-start(f32[64,128]{1,0:T(8,128)S(1)} %add.20), channel_id=1, source_target_pairs={{0,6},{1,7},{2,4},{3,5},{4,2},{5,3},{6,0},{7,1},{8,14},{9,15},{10,... | collective-permute-start | bytes 98312 | tf_op jit(solution)/shard_map/ppermute | solution.py:236
  43.3 0.5 collective-permute-start.1
  43.8 0.3 collective-permute-done.2
  44.1 2.9 %collective-permute-done.3 = f32[64,128]{1,0:T(8,128)S(1)} collective-permute-done((f32[64,128]{1,0:T(8,128)S(1)}, f32[64,128]{1,0:T(8,128)S(1)}, u32[]{:S(2)}, u32[]{:S(2)}) %collective-permute-start.3) | collective-permute-done | bytes 32800 | tf_op jit(solution)/shard_map/ppermute | solution.py:236
  47.0 0.3 collective-permute-done.1
  47.3 1.7 %collective-permute-start.4 = (f32[64,128]{1,0:T(8,128)S(1)}, f32[64,128]{1,0:T(8,128)S(1)}, u32[]{:S(2)}, u32[]{:S(2)}) collective-permute-start(f32[64,128]{1,0:T(8,128)S(1)} %add_add_fusion.refs_0_), channel_id=1, source_target_pairs={{0,8},{1,9},{2,10},{3,11},{4,12},{5,13},{6,14},{7,15},{8,0},{9,1},... | collective-permute-start | bytes 98312 | tf_op jit(solution)/shard_map/ppermute | solution.py:236
  49.1 0.0 copy-done.1
  49.1 0.1 reshape.36
  49.2 0.1 broadcast_in_dim.2
  49.2 0.1 reshape.37.refs_3_
  49.3 2.9 %collective-permute-done.4.refs_1_ = f32[64,128]{1,0:T(8,128)S(1)} collective-permute-done((f32[64,128]{1,0:T(8,128)S(1)}, f32[64,128]{1,0:T(8,128)S(1)}, u32[]{:S(2)}, u32[]{:S(2)}) %collective-permute-start.4) | collective-permute-done | bytes 32800 | tf_op jit(solution)/shard_map/ppermute | solution.py:236
  52.2 3.0 %shard_map.61 = (bf16[1024,256]{1,0:T(8,128)(2,1)}, f32[32,32,32]{2,1,0:T(8,128)}) custom-call(f32[64,128]{1,0:T(8,128)S(1)} %add_add_fusion.refs_0_, f32[64,128]{1,0:T(8,128)S(1)} %collective-permute-done.4.refs_1_, bf16[1024,256]{1,0:T(8,128)(2,1)S(1)} %get-tuple-element.7.refs_2_, s32[8,128]{1,0:T(8,128)S(1)} %reshape.37.refs_3_), custom_call_target="tpu_custom_call" | custom-call | tf_op jit(solution)/shard_map/pallas_call | solution.py:207
  (5 shorter events, 0.1 us)
Async XLA Ops:
  2.9 8.9 %copy-start = (s32[32]{0:T(128)S(1)}, s32[32]{0:T(128)}, u32[]{:S(2)}) copy-start(s32[32]{0:T(128)} %param.6) | copy-start | bytes 388
  2.9 9.1 %copy-start.2 = (s32[16]{0:T(128)S(1)}, s32[16]{0:T(128)}, u32[]{:S(2)}) copy-start(s32[16]{0:T(128)} %param.5) | copy-start | bytes 196
  2.9 31.5 %all-to-all-start = ((bf16[16,136,256]{2,1,0:T(8,128)(2,1)}), bf16[16,136,256]{2,1,0:T(8,128)(2,1)S(1)}, u32[]{:S(2)}, u32[]{:S(2)}) async-start(bf16[16,136,256]{2,1,0:T(8,128)(2,1)} %bitcast.8), calls=%async_computation | async-start | bytes 2228224 | tf_op jit(solution)/shard_map/all_to_all | solution.py:251
  13.0 36.1 %copy-start.1 = (s32[32]{0:T(128)S(1)}, s32[32]{0:T(128)}, u32[]{:S(2)}) copy-start(s32[32]{0:T(128)} %param.7) | copy-start | bytes 388
  37.0 1.6 %collective-permute-start = (f32[64,128]{1,0:T(8,128)S(1)}, f32[64,128]{1,0:T(8,128)S(1)}, u32[]{:S(2)}, u32[]{:S(2)}) collective-permute-start(f32[64,128]{1,0:T(8,128)S(1)} %get-tuple-element.6), channel_id=1, source_target_pairs={{0,1},{1,0},{2,3},{3,2},{4,5},{5,4},{6,7},{7,6},{8,9},{9,8},{10,11... | collective-permute-start | bytes 98312 | tf_op jit(solution)/shard_map/ppermute | solution.py:236
  38.6 5.4 %collective-permute-start.2 = (f32[64,128]{1,0:T(8,128)S(1)}, f32[64,128]{1,0:T(8,128)S(1)}, u32[]{:S(2)}, u32[]{:S(2)}) collective-permute-start(f32[64,128]{1,0:T(8,128)S(1)} %add.20), channel_id=1, source_target_pairs={{0,4},{1,5},{2,6},{3,7},{4,0},{5,1},{6,2},{7,3},{8,12},{9,13},{10,... | collective-permute-start | bytes 98312 | tf_op jit(solution)/shard_map/ppermute | solution.py:236
  42.2 4.8 %collective-permute-start.3 = (f32[64,128]{1,0:T(8,128)S(1)}, f32[64,128]{1,0:T(8,128)S(1)}, u32[]{:S(2)}, u32[]{:S(2)}) collective-permute-start(f32[64,128]{1,0:T(8,128)S(1)} %add.20), channel_id=1, source_target_pairs={{0,6},{1,7},{2,4},{3,5},{4,2},{5,3},{6,0},{7,1},{8,14},{9,15},{10,... | collective-permute-start | bytes 98312 | tf_op jit(solution)/shard_map/ppermute | solution.py:236
  43.3 4.0 %collective-permute-start.1 = (f32[64,128]{1,0:T(8,128)S(1)}, f32[64,128]{1,0:T(8,128)S(1)}, u32[]{:S(2)}, u32[]{:S(2)}) collective-permute-start(f32[64,128]{1,0:T(8,128)S(1)} %add.20), channel_id=1, source_target_pairs={{0,2},{1,3},{2,0},{3,1},{4,6},{5,7},{6,4},{7,5},{8,10},{9,11},{10,... | collective-permute-start | bytes 98312 | tf_op jit(solution)/shard_map/ppermute | solution.py:236
  47.3 4.9 %collective-permute-start.4 = (f32[64,128]{1,0:T(8,128)S(1)}, f32[64,128]{1,0:T(8,128)S(1)}, u32[]{:S(2)}, u32[]{:S(2)}) collective-permute-start(f32[64,128]{1,0:T(8,128)S(1)} %add_add_fusion.refs_0_), channel_id=1, source_target_pairs={{0,8},{1,9},{2,10},{3,11},{4,12},{5,13},{6,14},{7,15},{8,0},{9,1},... | collective-permute-start | bytes 98312 | tf_op jit(solution)/shard_map/ppermute | solution.py:236
